TPU v7x, 256 devices: a whole 4x4x8 slice. The times are simulated.
256 devices in a mesh: dp: 32 (over y, x, core), tensor: 8 (over z).
Axes of the slice: x: 4, y: 4, z: 8, core: 2. Of those that a mesh axis runs over, the one named last changes fastest.
Arguments:
- patches: bfloat16 [16384, 1280], P('dp'), may hold values from -6 to 6
- window_ids: int32 [32, 512], P('dp'), may hold values from 0 to 15, never falling along the last dimension, each value on 1 to 64 neighbouring positions
- vit_gain: float32 [1280], replicated, may hold values from 0.5 to 2
- qkv_weight: bfloat16 [3, 1280, 1280], P(None, None, 'tensor'), may hold values from -0.15625 to 0.15625
- out_weight: bfloat16 [1280, 1280], P('tensor'), may hold values from -0.15625 to 0.15625
- merge_gain: float32 [1280], replicated, may hold values from 0.5 to 2
- merger_weight: bfloat16 [5120, 3584], P(None, 'tensor'), may hold values from -0.078125 to 0.078125
- audio: bfloat16 [12288, 3584], P('dp', 'tensor'), may hold values from -6 to 6
- span_lengths: int32 [32, 32], replicated, may hold values from 8 to 32, as said below
- span_time: int32 [32, 32], replicated, may hold values from 0 to 31, each once within a row
- llm_gain: float32 [3584], replicated, may hold values from 0.5 to 2
- gate_weight: bfloat16 [3584, 9472], P('dp', 'tensor'), may hold values from -0.09375 to 0.09375
- up_weight: bfloat16 [3584, 9472], P('dp', 'tensor'), may hold values from -0.09375 to 0.09375
- down_weight: bfloat16 [9472, 3584], P('tensor', 'dp'), may hold values from -0.0625 to 0.0625
Outputs:
- mixed: bfloat16 [16384, 3584], P(('dp', 'tensor'))
Inputs may be any that keep to these rules, and one draw needn't show every extreme that they name: `span_lengths`: every row and every column sums to 512; every row and every column holds the value 32 at least once. `span_time`: each row is a permutation of the owners' numbers. `window_ids`: window numbers never fall along a row; a window holds at most 64 patches.
All inputs are finite; a program needn't handle non-finite values.
Results may differ from a plain program's by a relative error of at most 0.017.
Values may be sent and summed in bfloat16 or wider, within the bound.
No kernel may reach another device: no remote copies, remote signals or barrier semaphores. Data moves between devices by JAX's collectives and lax.ppermute only.
A program may use at most 128 MiB of HBM per device.

v0:
```python
import math
import jax
import jax.numpy as jnp
from jax import lax
from jax.sharding import PartitionSpec as P

D_VIT = 1280
HEAD_VIT = 80
EPSILON = 1e-06


def in_blocks(x, dim, devices):
    before, after = (x.shape[:dim], x.shape[dim + 1 :])
    return jnp.moveaxis(x.reshape(*before, devices, -1, *after), dim, 0)


def sent_and_summed(x, axis, dim):
    parts = in_blocks(x, dim, lax.axis_size(axis))
    arrived = lax.all_to_all(parts, axis, split_axis=0, concat_axis=0, tiled=True)
    return arrived.astype(jnp.float32).sum(axis=0)


def from_everyone(x, axis):
    devices = lax.axis_size(axis)
    return lax.all_to_all(jnp.broadcast_to(x[None], (devices, *x.shape)), axis, 0, 0, tiled=True)


def in_order(parts, dim):
    parts = jnp.moveaxis(parts, 0, dim)
    dims = parts.shape
    return parts.reshape(*dims[:dim], dims[dim] * dims[dim + 1], *dims[dim + 2 :])


def gather_directly(x, axis, dim):
    parts = from_everyone(x, axis)
    return in_order(parts, dim)


def gather_turned(arrays, axis, dims):
    turned = [jnp.moveaxis(a, dim, 0) for a, dim in zip(arrays, dims)]
    widths = [t[0].size for t in turned]
    both = jnp.concatenate([t.reshape(-1, w) for t, w in zip(turned, widths)], axis=1)
    whole = lax.all_gather(both, axis, axis=0, tiled=True)
    parts = jnp.split(whole, [sum(widths[:k]) for k in range(1, len(widths))], axis=1)
    return tuple(
        (
            jnp.moveaxis(b.reshape(-1, *t.shape[1:]), 0, dim)
            for b, t, dim in zip(parts, turned, dims)
        )
    )


def rms_scale(values, gain):
    wide = values.astype(jnp.float32)
    meansq = jnp.mean(wide * wide, axis=-1, keepdims=True)
    return wide * lax.rsqrt(meansq + EPSILON) * gain


def body(
    patches,
    window_ids,
    vit_gain,
    qkv_weight,
    out_weight,
    merge_gain,
    merger_weight,
    audio,
    span_lengths,
    span_time,
    llm_gain,
    gate_weight,
    up_weight,
    down_weight,
):
    patch_count = patches.shape[0]
    heads_here = qkv_weight.shape[2] // HEAD_VIT
    normed = rms_scale(patches, vit_gain).astype(jnp.bfloat16)
    query = jnp.dot(normed, qkv_weight[0], preferred_element_type=jnp.float32).astype(jnp.bfloat16)
    keys = jnp.dot(normed, qkv_weight[1], preferred_element_type=jnp.float32).astype(jnp.bfloat16)
    values = jnp.dot(normed, qkv_weight[2], preferred_element_type=jnp.float32).astype(jnp.bfloat16)
    query = query.reshape(patch_count, heads_here, HEAD_VIT)
    keys = keys.reshape(patch_count, heads_here, HEAD_VIT)
    values = values.reshape(patch_count, heads_here, HEAD_VIT)
    scores = jnp.einsum(
        "phe,qhe->hpq", query, keys, preferred_element_type=jnp.float32
    ) / math.sqrt(HEAD_VIT)
    windows = window_ids[0]
    same = windows[:, None] == windows[None, :]
    scores = jnp.where(same[None], scores, -1e30)
    probs = jax.nn.softmax(scores, axis=-1).astype(jnp.bfloat16)
    context = jnp.einsum("hpq,qhe->phe", probs, values, preferred_element_type=jnp.float32).astype(
        jnp.bfloat16
    )
    context = context.reshape(patch_count, heads_here * HEAD_VIT)
    partial_value = jnp.dot(context, out_weight, preferred_element_type=jnp.float32)
    share = sent_and_summed(partial_value.astype(jnp.bfloat16), "tensor", 0)
    share_rows = share.shape[0]
    own_frames = lax.dynamic_slice_in_dim(
        patches, lax.axis_index("tensor") * share_rows, share_rows, 0
    )
    own_encoded = (own_frames.astype(jnp.float32) + share).astype(jnp.bfloat16)
    encoded = gather_directly(own_encoded, "tensor", 0)
    merged = (
        rms_scale(encoded, merge_gain).astype(jnp.bfloat16).reshape(patch_count // 4, 4 * D_VIT)
    )
    video = jnp.dot(merged, merger_weight, preferred_element_type=jnp.float32).astype(jnp.bfloat16)
    source = jnp.concatenate([video, audio], axis=0)
    seq_count = source.shape[0]
    owner_count = lax.axis_size("dp")
    owner = lax.axis_index("dp")
    capacity = 2 * seq_count // owner_count
    sent_lengths = span_lengths[owner]
    starts = jnp.cumsum(sent_lengths) - sent_lengths
    slot_index = jnp.arange(capacity, dtype=jnp.int32)
    occupied = slot_index[None, :] < sent_lengths[:, None]
    source_index = jnp.where(occupied, starts[:, None] + slot_index[None, :], 0).reshape(-1)
    outgoing = jnp.take(source, source_index, axis=0)
    outgoing = jnp.where(occupied.reshape(-1)[:, None], outgoing, jnp.zeros((), outgoing.dtype))
    incoming = lax.all_to_all(outgoing, "dp", split_axis=0, concat_axis=0, tiled=True)
    taken_lengths = span_lengths[:, owner]
    arrival = span_time[owner]
    earlier = arrival[:, None] < arrival[None, :]
    offsets = jnp.sum(jnp.where(earlier, taken_lengths[:, None], 0), axis=0)
    position = jnp.arange(seq_count, dtype=jnp.int32)
    inside = (position[None, :] >= offsets[:, None]) & (
        position[None, :] < offsets[:, None] + taken_lengths[:, None]
    )
    sender = jnp.arange(owner_count, dtype=jnp.int32)[:, None]
    slot_row = sender * capacity + position[None, :] - offsets[:, None]
    picked = jnp.sum(jnp.where(inside, slot_row, 0), axis=0)
    sequence = jnp.take(incoming, picked, axis=0)
    features = lax.all_gather(sequence, "tensor", axis=1, tiled=True)
    normed_seq = rms_scale(features, llm_gain).astype(jnp.bfloat16)
    gate_full, up_full, down_full = gather_turned(
        (gate_weight, up_weight, down_weight), "dp", (0, 0, 1)
    )
    gate = jnp.dot(normed_seq, gate_full, preferred_element_type=jnp.float32)
    upward = jnp.dot(normed_seq, up_full, preferred_element_type=jnp.float32)
    hidden = (jax.nn.silu(gate) * upward).astype(jnp.bfloat16)
    terms = jnp.dot(hidden, down_full, preferred_element_type=jnp.float32)
    summed = lax.psum_scatter(
        terms.astype(jnp.bfloat16), "tensor", scatter_dimension=0, tiled=True
    ).astype(jnp.float32)
    own_count = summed.shape[0]
    own_rows = lax.dynamic_slice_in_dim(
        features, lax.axis_index("tensor") * own_count, own_count, 0
    )
    return (own_rows.astype(jnp.float32) + summed).astype(jnp.bfloat16)


def solution(mesh):
    return jax.shard_map(
        body,
        mesh=mesh,
        in_specs=(
            P("dp", None),
            P("dp", None),
            P(),
            P(None, None, "tensor"),
            P("tensor", None),
            P(),
            P(None, "tensor"),
            P("dp", "tensor"),
            P(),
            P(),
            P(),
            P("dp", "tensor"),
            P("dp", "tensor"),
            P("tensor", "dp"),
        ),
        out_specs=P(("dp", "tensor"), None),
        check_vma=False,
    )
```

profile of v0, /device:TPU:1, one launch (start us, length us, event | category | flops | bytes accessed | tf_op | source)
XLA Modules:
  0.0 377.8 jit_solution(1047735685525039576)
XLA Ops:
  6.5 1.8 fusion.19
  8.4 2.1 convolution_convert_fusion.3
  10.5 0.7 convolution_convert_fusion.2
  11.1 0.7 convolution_convert_fusion.4
  11.8 0.2 broadcast_compare_fusion
  12.0 1.0 fusion.61
  13.0 1.2 convolution_convert_fusion.1
  14.3 1.6 convolution_convert_fusion
  15.9 9.0 %all-to-all-start = ((bf16[8,64,1280]{2,1,0:T(8,128)(2,1)}), bf16[8,64,1280]{2,1,0:T(8,128)(2,1)S(1)}, u32[]{:S(2)}, u32[]{:S(2)}) async-start(bf16[8,64,1280]{2,1,0:T(8,128)(2,1)} %bitcast.15), calls=%async_computation | async-start | bytes 2621440 | tf_op jit(solution)/shard_map/all_to_all | solution.py:19
  24.9 34.9 %all-to-all-done = bf16[8,64,1280]{2,1,0:T(8,128)(2,1)S(1)} async-done(((bf16[8,64,1280]{2,1,0:T(8,128)(2,1)}), bf16[8,64,1280]{2,1,0:T(8,128)(2,1)S(1)}, u32[]{:S(2)}, u32[]{:S(2)}) %all-to-all-start) | async-done | bytes 1310752 | tf_op jit(solution)/shard_map/all_to_all | solution.py:19
  59.8 0.2 convert_reduce_fusion
  60.1 1.1 broadcast_in_dim.103
  61.2 3.6 all-to-all-start.1
  64.8 0.2 copy.36
  65.1 0.1 copy.33
  65.2 0.1 reduce.1
  65.4 0.1 select_n.94
  65.6 0.1 copy.40
  65.7 0.7 fusion.44
  66.4 0.1 select_reduce_fusion.1
  66.5 0.1 iota_compare_fusion.2
  66.6 32.9 %all-to-all-done.1 = bf16[8,64,1280]{2,1,0:T(8,128)(2,1)S(1)} async-done(((bf16[8,64,1280]{2,1,0:T(8,128)(2,1)}), bf16[8,64,1280]{2,1,0:T(8,128)(2,1)S(1)}, u32[]{:S(2)}, u32[]{:S(2)}) %all-to-all-start.1) | async-done | bytes 1310752 | tf_op jit(solution)/shard_map/all_to_all | solution.py:25
  99.5 0.3 multiply_reduce_fusion
  99.9 0.1 rsqrt.29
  100.0 0.4 mul.97
  100.4 2.0 copy.42
  102.3 1.9 reshape.242
  104.2 5.2 %fusion.25 = bf16[128,448]{0,1:T(8,128)(2,1)S(1)} fusion(bf16[5120,448]{0,1:T(8,128)(2,1)} %param.20, f32[128,5120]{1,0:T(8,128)} %reshape.242, f32[128,5120]{1,0:T(8,128)} %bitcast.49, f32[5120]{0:T(1024)S(1)} %mul.101), kind=kOutput, calls=%fused_computation.36 | convolution fusion | flops 589225984 | bytes 9965568 | tf_op jit(solution)/shard_map/dot_general | solution.py:106
  109.4 0.1 copy.35
  109.6 4.0 %gather_fusion = bf16[1024,448]{1,0:T(8,128)(2,1)S(1)} fusion(bf16[512,448]{1,0:T(8,128)(2,1)S(1)} %pad_maximum_fusion, s32[1024]{0:T(1024)S(1)} %broadcast_clamp_fusion), kind=kCustom, calls=%fused_computation | custom fusion | bytes 1839104 | tf_op jit(solution)/shard_map/jit(_take)/gather | solution.py:117
  113.6 1.3 select_select_fusion
  114.9 7.6 %all-to-all-start.2 = ((bf16[32,32,448]{2,1,0:T(8,128)(2,1)}), bf16[32,32,448]{2,1,0:T(8,128)(2,1)S(1)}, u32[]{:S(2)}, u32[]{:S(2)}) async-start(bf16[32,32,448]{2,1,0:T(8,128)(2,1)} %select_select_fusion), calls=%async_computation.2 | async-start | bytes 2097152 | tf_op jit(solution)/shard_map/all_to_all | solution.py:119
  122.5 0.1 select_reduce_fusion
  122.6 17.0 %all-to-all-done.2 = bf16[32,32,448]{2,1,0:T(8,128)(2,1)S(1)} async-done(((bf16[32,32,448]{2,1,0:T(8,128)(2,1)}), bf16[32,32,448]{2,1,0:T(8,128)(2,1)S(1)}, u32[]{:S(2)}, u32[]{:S(2)}) %all-to-all-start.2) | async-done | bytes 917536 | tf_op jit(solution)/shard_map/all_to_all | solution.py:119
  139.6 2.0 gather_fusion.1
  141.6 0.1 broadcast_select_fusion
  141.7 1.0 copy.37
  142.8 1.4 concatenate.7
  144.2 0.2 reduce-scatter.2.cloned.1.call-start
  144.4 40.7 %all-gather.3.cloned.1.call-done = bf16[512,3584]{0,1:T(8,128)(2,1)} async-done(((bf16[512,448]{0,1:T(8,128)(2,1)}), bf16[512,3584]{0,1:T(8,128)(2,1)}) %all-gather.3.cloned.1.call-update) | async-done | bytes 3670032 | tf_op jit(solution)/shard_map/all_gather | solution.py:132
  185.1 2.9 fusion.7
  188.0 97.1 %all-gather.5.cloned.1.call-done = bf16[3584,3552]{1,0:T(8,128)(2,1)} async-done(((bf16[112,3552]{1,0:T(8,128)(2,1)}), bf16[3584,3552]{1,0:T(8,128)(2,1)}) %all-gather.5.cloned.1.call-update) | async-done | bytes 25460752 | tf_op jit(solution)/shard_map/all_gather | solution.py:43
  285.1 9.8 %fusion.5 = f32[512,1184]{0,1:T(8,128)S(1)} fusion(bf16[3584,3552]{1,0:T(8,128)(2,1)} %all-gather.5.cloned.1.call-done, bf16[512,3584]{0,1:T(8,128)(2,1)} %all-gather.3.cloned.1.call-done, f32[3584]{0:T(1024)S(1)} %copy-done.11, f32[512]{0:T(512)S(1)} %add_rsqrt_fusion.1), kind=kOutput, calls=%fused_computation.7 | convolution fusion | flops 4352638976 | bytes 15286272 | tf_op jit(solution)/shard_map/dot_general | solution.py:137
  294.9 24.9 %fusion.10 = bf16[512,3584]{1,0:T(8,128)(2,1)} fusion(bf16[3584,3552]{1,0:T(8,128)(2,1)} %all-gather.5.cloned.1.call-done, f32[512,1184]{0,1:T(8,128)S(1)} %fusion.5, bf16[512,3584]{0,1:T(8,128)(2,1)} %all-gather.3.cloned.1.call-done, f32[3584]{0:T(1024)S(1)} %copy-done.11, f32[512]{0:T(512)S(1)} %add_rsqrt_fusion.1), kind=kOutput, calls=%fused_computation.14 | convolution fusion | flops 8703410176 | bytes 28131328 | tf_op jit(solution)/shard_map/dot_general | solution.py:140
  319.8 1.6 constant_dynamic-slice_fusion
  321.4 0.3 copy.41
  321.7 47.7 %reduce-scatter.2.cloned.1.call-done = bf16[64,3584]{1,0:T(8,128)(2,1)} async-done(((bf16[512,3584]{1,0:T(8,128)(2,1)}), bf16[64,3584]{1,0:T(8,128)(2,1)}) %reduce-scatter.2.cloned.1.call-update) | async-done | bytes 458768 | tf_op jit(solution)/shard_map/reduce_scatter | solution.py:141
  369.4 1.9 add_convert_fusion
  (50 shorter events, 0.6 us)
Async XLA Ops:
  6.5 7.7 %copy-start = (bf16[160,1280]{1,0:T(8,128)(2,1)S(1)}, bf16[160,1280]{1,0:T(8,128)(2,1)}, u32[]{:S(2)}) copy-start(bf16[160,1280]{1,0:T(8,128)(2,1)} %param.18) | copy-start | bytes 1228804
  6.5 3.9 %copy-start.2 = (bf16[512,1280]{1,0:T(8,128)(2,1)S(1)}, bf16[512,1280]{1,0:T(8,128)(2,1)}, u32[]{:S(2)}) copy-start(bf16[512,1280]{1,0:T(8,128)(2,1)} %param.14) | copy-start | bytes 3932164
  6.5 3.9 %copy-start.12 = (f32[1280]{0:T(1024)S(1)}, f32[1280]{0:T(1024)}, u32[]{:S(2)}) copy-start(f32[1280]{0:T(1024)} %param.16) | copy-start | bytes 15364
  6.5 3.9 %copy-start.10 = (bf16[3,1280,160]{1,2,0:T(8,128)(2,1)S(1)}, bf16[3,1280,160]{1,2,0:T(8,128)(2,1)}, u32[]{:S(2)}) copy-start(bf16[3,1280,160]{1,2,0:T(8,128)(2,1)} %param.17) | copy-start | bytes 3686404
  10.5 1.3 copy-start.8
  15.9 43.9 %all-to-all-start = ((bf16[8,64,1280]{2,1,0:T(8,128)(2,1)}), bf16[8,64,1280]{2,1,0:T(8,128)(2,1)S(1)}, u32[]{:S(2)}, u32[]{:S(2)}) async-start(bf16[8,64,1280]{2,1,0:T(8,128)(2,1)} %bitcast.15), calls=%async_computation | async-start | bytes 2621440 | tf_op jit(solution)/shard_map/all_to_all | solution.py:19
  60.0 4.8 %copy-start.9 = (f32[1280]{0:T(1024)S(1)}, f32[1280]{0:T(1024)}, u32[]{:S(2)}) copy-start(f32[1280]{0:T(1024)} %param.19) | copy-start | bytes 15364
  60.0 4.8 %copy-start.3 = (bf16[384,448]{0,1:T(8,128)(2,1)S(1)}, bf16[384,448]{0,1:T(8,128)(2,1)}, u32[]{:S(2)}) copy-start(bf16[384,448]{0,1:T(8,128)(2,1)} %param.21) | copy-start | bytes 1032196
  60.0 5.0 %copy-start.7 = (s32[32,32]{1,0:T(8,128)S(1)}, s32[32,32]{1,0:T(8,128)}, u32[]{:S(2)}) copy-start(s32[32,32]{1,0:T(8,128)} %param.22) | copy-start | bytes 12292
  61.2 38.3 %all-to-all-start.1 = ((bf16[8,64,1280]{2,1,0:T(8,128)(2,1)}), bf16[8,64,1280]{2,1,0:T(8,128)(2,1)S(1)}, u32[]{:S(2)}, u32[]{:S(2)}) async-start(bf16[8,64,1280]{2,1,0:T(8,128)(2,1)} %broadcast_in_dim.103), calls=%async_computation.1 | async-start | bytes 2621440 | tf_op jit(solution)/shard_map/all_to_all | solution.py:25
  114.9 24.8 %all-to-all-start.2 = ((bf16[32,32,448]{2,1,0:T(8,128)(2,1)}), bf16[32,32,448]{2,1,0:T(8,128)(2,1)S(1)}, u32[]{:S(2)}, u32[]{:S(2)}) async-start(bf16[32,32,448]{2,1,0:T(8,128)(2,1)} %select_select_fusion), calls=%async_computation.2 | async-start | bytes 2097152 | tf_op jit(solution)/shard_map/all_to_all | solution.py:119
  122.4 62.7 %all-gather.3.cloned.1.call-start = ((), (), s32[]{:S(2)}) async-start(), calls=%async_computation.4 | async-start | bytes 4128768 | tf_op jit(solution)/shard_map/all_gather | solution.py:132
  139.6 3.2 copy-start.4
  139.6 3.2 copy-start.5
  139.6 3.2 copy-start.6
  142.7 142.4 %all-gather.5.cloned.1.call-start = ((), (), s32[]{:S(2)}) async-start(), calls=%async_computation.5 | async-start | bytes 26492928 | tf_op jit(solution)/shard_map/all_gather | solution.py:43
  144.1 141.0 %copy-start.11 = (f32[3584]{0:T(1024)S(1)}, f32[3584]{0:T(1024)}, u32[]{:S(2)}) copy-start(f32[3584]{0:T(1024)} %param.24) | copy-start | bytes 43012
  144.2 225.2 %reduce-scatter.2.cloned.1.call-start = ((), (), s32[]{:S(2)}) async-start(), calls=%async_computation.6 | async-start | bytes 4128768 | tf_op jit(solution)/shard_map/reduce_scatter | solution.py:141
  319.8 51.5 %copy-start.1 = (bf16[160,1280]{1,0:T(8,128)(2,1)S(1)}, bf16[160,1280]{1,0:T(8,128)(2,1)}, u32[]{:S(2)}) copy-start(bf16[160,1280]{1,0:T(8,128)(2,1)} %param.18) | copy-start | bytes 1228804
Sparse Core Ops, SparseCore 0:
  142.8 42.2 all-gather.2
  187.7 97.3 all-gather.4
  319.9 49.4 reduce-scatter.1
where the time goes:
time: 378 us
  waiting for transfers between devices  270 us (71%)
  matrix products  47.1 us (12%)
  starting transfers between devices  20.5 us (5%)
  local copies, waits for them, and re-layouts  17 us (4%)
  between operations  13.5 us (4%)
  other arithmetic  9.35 us (2%)
    all_gather x1, waiting for transfers between devices, gather_turned(): whole = lax.all_gather(both, axis, axis=0, tiled=True)  97.1 us
    reduce_scatter x1, waiting for transfers between devices, body(): lax.psum_scatter(terms.astype(jnp.bfloat16), 'tensor', scatter_dimension=...  47.7 us
    all_gather x1, waiting for transfers between devices, body(): features = lax.all_gather(sequence, 'tensor', axis=1, tiled=True)  40.7 us
    all_to_all x1, waiting for transfers between devices, sent_and_summed(): lax.all_to_all(parts, axis, split_axis=0, concat_axis=0, tiled=True)  34.9 us
    all_to_all x1, waiting for transfers between devices, from_everyone(): lax.all_to_all(jnp.broadcast_to(x[None], (devices, *x.shape)), axis, 0, 0...  32.9 us
    dot_general x1, matrix products, body(): terms = jnp.dot(hidden, down_full, preferred_element_type=jnp.float32)  24.9 us
    all_to_all x1, waiting for transfers between devices, body(): lax.all_to_all(outgoing, 'dp', split_axis=0, concat_axis=0, tiled=True)  17 us
    dot_general x1, matrix products, body(): gate = jnp.dot(normed_seq, gate_full, preferred_element_type=jnp.float32)  9.77 us
  transfers between devices with their start and end apart: 6, of which 6 were waited for; matrix products, arithmetic and copies ran while one was open for 2% of the time, Pallas kernels for 0%

commit v1 on v0

--- a/solution.py
+++ b/solution.py
@@ -72,6 +72,20 @@
     up_weight,
     down_weight,
 ):
+
+    def drive_record_up(group_axis, in_array):
+        extent = lax.axis_size(group_axis)
+        r1 = [(ix - 1, ix) for ix in range(1, extent)] + [(extent - 1, 0)]
+        top = in_array
+        store = [top]
+        i0 = 0
+        while i0 < extent - 1:
+            top = lax.ppermute(top, group_axis, r1)
+            store += [top]
+            i0 += 1
+        now = jnp.concatenate([*reversed(store)], axis=1)
+        return jnp.roll(now, (lax.axis_index(group_axis) + 1) * top.shape[1], axis=1)
+
     patch_count = patches.shape[0]
     heads_here = qkv_weight.shape[2] // HEAD_VIT
     normed = rms_scale(patches, vit_gain).astype(jnp.bfloat16)
@@ -129,7 +143,7 @@
     slot_row = sender * capacity + position[None, :] - offsets[:, None]
     picked = jnp.sum(jnp.where(inside, slot_row, 0), axis=0)
     sequence = jnp.take(incoming, picked, axis=0)
-    features = lax.all_gather(sequence, "tensor", axis=1, tiled=True)
+    features = drive_record_up("tensor", sequence)
     normed_seq = rms_scale(features, llm_gain).astype(jnp.bfloat16)
     gate_full, up_full, down_full = gather_turned(
         (gate_weight, up_weight, down_weight), "dp", (0, 0, 1)

time: 378 us -> 349 us (0.923)
  waiting for transfers between devices: 270 us -> 221 us
  local copies, waits for them, and re-layouts: 17 us -> 27 us
  matrix products: 47.1 us -> 54.3 us
    all_gather x1, waiting for transfers between devices: 97.1 us -> 0.02 us  [gather_turned(): whole = lax.all_gather(both, axis, axis=0, tiled=True)]
    ppermute x0 -> x7, waiting for transfers between devices: none -> 83.3 us  [drive_record_up(): top = lax.ppermute(top, group_axis, r1)]
    all_gather x1 -> x0, waiting for transfers between devices: 40.7 us -> none  [body(): features = lax.all_gather(sequence, 'tensor', axis=1, tiled=True)]
    dot_general x0 -> x1, matrix products: none -> 14.2 us  [body(): upward = jnp.dot(normed_seq, up_full, preferred_element_type=jnp.float32)]
    concatenate x0 -> x1, local copies, waits for them, and re-layouts: none -> 11.6 us  [drive_record_up(): jnp.roll(now, (lax.axis_index(group_axis) + 1) * top.shape[1], axis=1)]
    dot_general x1, matrix products: 24.9 us -> 15.8 us  [body(): terms = jnp.dot(hidden, down_full, preferred_element_type=jnp.float32)]
    reduce_scatter x1, waiting for transfers between devices: 47.7 us -> 52.8 us  [body(): lax.psum_scatter(terms.astype(jnp.bfloat16), 'tensor', scatter_dimension=...]
  transfers between devices with their start and end apart: 6 -> 12, of which waited for: 6 -> 11; matrix products, arithmetic and copies ran while one was open for 2% -> 14% of each run, Pallas kernels for 0% -> 0%
where the time goes in v1:
time: 349 us; the launch traced here: 347 us
  waiting for transfers between devices  221 us (63%)
  matrix products  54.3 us (16%)
  local copies, waits for them, and re-layouts  27 us (8%)
  starting transfers between devices  20.9 us (6%)
  between operations  13.8 us (4%)
  other arithmetic  10.5 us (3%)
    ppermute x7, waiting for transfers between devices, drive_record_up(): top = lax.ppermute(top, group_axis, r1)  83.3 us
    reduce_scatter x1, waiting for transfers between devices, body(): lax.psum_scatter(terms.astype(jnp.bfloat16), 'tensor', scatter_dimension=...  52.8 us
    all_to_all x1, waiting for transfers between devices, sent_and_summed(): lax.all_to_all(parts, axis, split_axis=0, concat_axis=0, tiled=True)  34.9 us
    all_to_all x1, waiting for transfers between devices, from_everyone(): lax.all_to_all(jnp.broadcast_to(x[None], (devices, *x.shape)), axis, 0, 0...  33 us
    all_to_all x1, waiting for transfers between devices, body(): lax.all_to_all(outgoing, 'dp', split_axis=0, concat_axis=0, tiled=True)  17 us
    dot_general x1, matrix products, body(): terms = jnp.dot(hidden, down_full, preferred_element_type=jnp.float32)  15.8 us
    dot_general x1, matrix products, body(): upward = jnp.dot(normed_seq, up_full, preferred_element_type=jnp.float32)  14.2 us
    concatenate x1, local copies, waits for them, and re-layouts, drive_record_up(): jnp.roll(now, (lax.axis_index(group_axis) + 1) * top.shape[1], axis=1)  11.6 us
  transfers between devices with their start and end apart: 12, of which 11 were waited for; matrix products, arithmetic and copies ran while one was open for 14% of the time, Pallas kernels for 0%

profile of v1, /device:TPU:1, one launch (start us, length us, event | category | flops | bytes accessed | tf_op | source)
XLA Modules:
  0.0 347.4 jit_solution(16510061851415440405)
XLA Ops:
  6.6 2.4 concatenate.14
  9.0 0.3 fusion.13
  9.4 0.2 broadcast_compare_fusion
  9.6 1.7 convolution_convert_fusion.3
  11.3 1.7 convolution_convert_fusion.2
  12.9 1.0 fusion.54
  13.9 1.7 convolution_convert_fusion.4
  15.6 1.2 convolution_convert_fusion.1
  16.9 1.7 convolution_convert_fusion
  18.5 9.0 %all-to-all-start = ((bf16[8,64,1280]{2,1,0:T(8,128)(2,1)}), bf16[8,64,1280]{2,1,0:T(8,128)(2,1)S(1)}, u32[]{:S(2)}, u32[]{:S(2)}) async-start(bf16[8,64,1280]{2,1,0:T(8,128)(2,1)} %bitcast.15), calls=%async_computation | async-start | bytes 2621440 | tf_op jit(solution)/shard_map/all_to_all | solution.py:19
  27.5 34.9 %all-to-all-done = bf16[8,64,1280]{2,1,0:T(8,128)(2,1)S(1)} async-done(((bf16[8,64,1280]{2,1,0:T(8,128)(2,1)}), bf16[8,64,1280]{2,1,0:T(8,128)(2,1)S(1)}, u32[]{:S(2)}, u32[]{:S(2)}) %all-to-all-start) | async-done | bytes 1310752 | tf_op jit(solution)/shard_map/all_to_all | solution.py:19
  62.4 0.2 convert_reduce_fusion
  62.7 1.2 broadcast_in_dim.103
  63.9 3.6 %all-to-all-start.1 = ((bf16[8,64,1280]{2,1,0:T(8,128)(2,1)}), bf16[8,64,1280]{2,1,0:T(8,128)(2,1)S(1)}, u32[]{:S(2)}, u32[]{:S(2)}) async-start(bf16[8,64,1280]{2,1,0:T(8,128)(2,1)} %broadcast_in_dim.103), calls=%async_computation.1 | async-start | bytes 2621440 | tf_op jit(solution)/shard_map/all_to_all | solution.py:25
  67.6 0.1 reduce.1
  68.1 0.2 copy.29
  68.3 0.7 fusion.37
  69.0 0.1 select_reduce_fusion.1
  69.2 33.0 %all-to-all-done.1 = bf16[8,64,1280]{2,1,0:T(8,128)(2,1)S(1)} async-done(((bf16[8,64,1280]{2,1,0:T(8,128)(2,1)}), bf16[8,64,1280]{2,1,0:T(8,128)(2,1)S(1)}, u32[]{:S(2)}, u32[]{:S(2)}) %all-to-all-start.1) | async-done | bytes 1310752 | tf_op jit(solution)/shard_map/all_to_all | solution.py:25
  102.2 0.3 multiply_reduce_fusion
  102.5 0.1 rsqrt.29
  102.6 0.4 mul.100
  103.0 2.0 copy.32
  105.1 1.9 reshape.242
  107.0 5.2 %fusion.20 = bf16[128,448]{0,1:T(8,128)(2,1)S(1)} fusion(bf16[5120,448]{0,1:T(8,128)(2,1)} %param.20, f32[128,5120]{1,0:T(8,128)} %reshape.242, f32[128,5120]{1,0:T(8,128)} %bitcast.49, f32[5120]{0:T(1024)S(1)} %mul.104), kind=kOutput, calls=%fused_computation.36 | convolution fusion | flops 589225984 | bytes 9965568 | tf_op jit(solution)/shard_map/dot_general | solution.py:120
  112.2 0.1 copy.28
  112.4 4.0 %gather_fusion = bf16[1024,448]{1,0:T(8,128)(2,1)S(1)} fusion(bf16[512,448]{1,0:T(8,128)(2,1)S(1)} %pad_maximum_fusion, s32[1024]{0:T(1024)S(1)} %broadcast_clamp_fusion), kind=kCustom, calls=%fused_computation | custom fusion | bytes 1839104 | tf_op jit(solution)/shard_map/jit(_take)/gather | solution.py:131
  116.4 1.3 select_select_fusion
  117.6 7.8 %all-to-all-start.2 = ((bf16[32,32,448]{2,1,0:T(8,128)(2,1)}), bf16[32,32,448]{2,1,0:T(8,128)(2,1)S(1)}, u32[]{:S(2)}, u32[]{:S(2)}) async-start(bf16[32,32,448]{2,1,0:T(8,128)(2,1)} %select_select_fusion), calls=%async_computation.2 | async-start | bytes 2097152 | tf_op jit(solution)/shard_map/all_to_all | solution.py:133
  125.5 0.1 select_reduce_fusion
  125.7 17.0 %all-to-all-done.2 = bf16[32,32,448]{2,1,0:T(8,128)(2,1)S(1)} async-done(((bf16[32,32,448]{2,1,0:T(8,128)(2,1)}), bf16[32,32,448]{2,1,0:T(8,128)(2,1)S(1)}, u32[]{:S(2)}, u32[]{:S(2)}) %all-to-all-start.2) | async-done | bytes 917536 | tf_op jit(solution)/shard_map/all_to_all | solution.py:133
  142.7 2.0 gather_fusion.1
  144.6 0.1 broadcast_select_fusion
  144.8 0.4 collective-permute-start
  145.1 14.0 %collective-permute-done = bf16[512,448]{1,0:T(8,128)(2,1)S(1)} collective-permute-done((bf16[512,448]{1,0:T(8,128)(2,1)S(1)}, bf16[512,448]{1,0:T(8,128)(2,1)S(1)}, u32[]{:S(2)}, u32[]{:S(2)}) %collective-permute-start) | collective-permute-done | bytes 458784 | tf_op jit(solution)/shard_map/ppermute | solution.py:83
  159.2 13.4 %collective-permute-done.1 = bf16[512,448]{1,0:T(8,128)(2,1)S(1)} collective-permute-done((bf16[512,448]{1,0:T(8,128)(2,1)S(1)}, bf16[512,448]{1,0:T(8,128)(2,1)S(1)}, u32[]{:S(2)}, u32[]{:S(2)}) %collective-permute-start.1) | collective-permute-done | bytes 458784 | tf_op jit(solution)/shard_map/ppermute | solution.py:83
  172.6 12.5 %collective-permute-done.2 = bf16[512,448]{1,0:T(8,128)(2,1)S(1)} collective-permute-done((bf16[512,448]{1,0:T(8,128)(2,1)S(1)}, bf16[512,448]{1,0:T(8,128)(2,1)S(1)}, u32[]{:S(2)}, u32[]{:S(2)}) %collective-permute-start.2) | collective-permute-done | bytes 458784 | tf_op jit(solution)/shard_map/ppermute | solution.py:83
  185.1 11.6 %collective-permute-done.3 = bf16[512,448]{1,0:T(8,128)(2,1)S(1)} collective-permute-done((bf16[512,448]{1,0:T(8,128)(2,1)S(1)}, bf16[512,448]{1,0:T(8,128)(2,1)S(1)}, u32[]{:S(2)}, u32[]{:S(2)}) %collective-permute-start.3) | collective-permute-done | bytes 458784 | tf_op jit(solution)/shard_map/ppermute | solution.py:83
  196.6 10.6 %collective-permute-done.4 = bf16[512,448]{1,0:T(8,128)(2,1)S(1)} collective-permute-done((bf16[512,448]{1,0:T(8,128)(2,1)S(1)}, bf16[512,448]{1,0:T(8,128)(2,1)S(1)}, u32[]{:S(2)}, u32[]{:S(2)}) %collective-permute-start.4) | collective-permute-done | bytes 458784 | tf_op jit(solution)/shard_map/ppermute | solution.py:83
  207.2 10.5 %collective-permute-done.5 = bf16[512,448]{1,0:T(8,128)(2,1)} collective-permute-done((bf16[512,448]{1,0:T(8,128)(2,1)S(1)}, bf16[512,448]{1,0:T(8,128)(2,1)}, u32[]{:S(2)}, u32[]{:S(2)}) %collective-permute-start.5) | collective-permute-done | bytes 458784 | tf_op jit(solution)/shard_map/ppermute | solution.py:83
  217.7 10.7 %collective-permute-done.6 = bf16[512,448]{1,0:T(8,128)(2,1)} collective-permute-done((bf16[512,448]{1,0:T(8,128)(2,1)}, bf16[512,448]{1,0:T(8,128)(2,1)}, u32[]{:S(2)}, u32[]{:S(2)}) %collective-permute-start.6) | collective-permute-done | bytes 458784 | tf_op jit(solution)/shard_map/ppermute | solution.py:83
  228.4 11.6 %concatenate.13 = bf16[512,7168]{1,0:T(8,128)(2,1)} concatenate(bf16[512,448]{1,0:T(8,128)(2,1)} %collective-permute-done.6, bf16[512,448]{1,0:T(8,128)(2,1)} %collective-permute-done.5, bf16[512,448]{1,0:T(8,128)(2,1)S(1)} %collective-permute-done.4, bf16[512,448]{1,0:T(8,128)(2,1)S(1)} %collective-permute-done.3, bf16[512,448]{1,0:T(8,128)(2,1)S(1)} %collective-permute-done.2, ...), dimensions={1} | concatenate | bytes 14680064 | tf_op jit(solution)/shard_map/jit(_roll_dynamic)/concatenate | solution.py:87
  240.0 5.2 %fusion.7 = f32[512]{0:T(512)S(1)} fusion(bf16[512,7168]{1,0:T(8,128)(2,1)} %concatenate.13, s32[]{:T(128)S(6)} %select_n.119), kind=kLoop, calls=%fused_computation.11 | loop fusion | flops 5504512 | bytes 3672068 | tf_op jit(solution)/shard_map/reduce_sum | solution.py:55
  245.3 14.2 %fusion.3 = f32[512,1184]{0,1:T(8,128)S(1)} fusion(bf16[3584,3552]{1,0:T(8,128)(2,1)} %all-gather.2.cloned.1.call-done, f32[3584]{0:T(1024)S(1)} %copy-done.7, f32[512]{0:T(512)S(1)} %add_rsqrt_fusion.1, bf16[512,7168]{1,0:T(8,128)(2,1)} %concatenate.13, s32[]{:T(128)S(6)} %select_n.119), kind=kOutput, calls=%fused_computation.5 | convolution fusion | flops 4352638976 | bytes 15286276 | tf_op jit(solution)/shard_map/dot_general | solution.py:152
  259.5 10.2 %fusion.5 = f32[512,1184]{0,1:T(8,128)S(1)} fusion(bf16[3584,3552]{1,0:T(8,128)(2,1)} %all-gather.2.cloned.1.call-done, f32[3584]{0:T(1024)S(1)} %copy-done.7, f32[512]{0:T(512)S(1)} %add_rsqrt_fusion.1, bf16[512,7168]{1,0:T(8,128)(2,1)} %concatenate.13, s32[]{:T(128)S(6)} %select_n.119), kind=kOutput, calls=%fused_computation.7 | convolution fusion | flops 4352638976 | bytes 15286276 | tf_op jit(solution)/shard_map/dot_general | solution.py:151
  269.7 15.8 %fusion.10 = bf16[512,3584]{1,0:T(8,128)(2,1)} fusion(bf16[3584,3552]{1,0:T(8,128)(2,1)} %all-gather.2.cloned.1.call-done, f32[512,1184]{0,1:T(8,128)S(1)} %fusion.3, f32[512,1184]{0,1:T(8,128)S(1)} %fusion.5), kind=kOutput, calls=%fused_computation.14 | convolution fusion | flops 4350771200 | bytes 17694720 | tf_op jit(solution)/shard_map/dot_general | solution.py:154
  285.6 52.8 %reduce-scatter.2.cloned.1.call-done = bf16[64,3584]{1,0:T(8,128)(2,1)} async-done(((bf16[512,3584]{1,0:T(8,128)(2,1)}), bf16[64,3584]{1,0:T(8,128)(2,1)}) %reduce-scatter.2.cloned.1.call-update) | async-done | bytes 458768 | tf_op jit(solution)/shard_map/reduce_scatter | solution.py:155
  338.4 2.2 add_convert_fusion
  (52 shorter events, 0.9 us)
Async XLA Ops:
  6.5 10.3 %copy-start = (bf16[160,1280]{1,0:T(8,128)(2,1)S(1)}, bf16[160,1280]{1,0:T(8,128)(2,1)}, u32[]{:S(2)}) copy-start(bf16[160,1280]{1,0:T(8,128)(2,1)} %param.18) | copy-start | bytes 1228804
  6.5 2.5 copy-start.2
  6.5 2.8 copy-start.5
  6.5 3.1 copy-start.8
  6.5 238.7 %all-gather.2.cloned.1.call-start = ((), (), s32[]{:S(2)}) async-start(), calls=%async_computation.4 | async-start | bytes 26492928 | tf_op jit(solution)/shard_map/all_gather | solution.py:43
  18.5 43.9 %all-to-all-start = ((bf16[8,64,1280]{2,1,0:T(8,128)(2,1)}), bf16[8,64,1280]{2,1,0:T(8,128)(2,1)S(1)}, u32[]{:S(2)}, u32[]{:S(2)}) async-start(bf16[8,64,1280]{2,1,0:T(8,128)(2,1)} %bitcast.15), calls=%async_computation | async-start | bytes 2621440 | tf_op jit(solution)/shard_map/all_to_all | solution.py:19
  62.6 4.9 %copy-start.4 = (s32[32,32]{1,0:T(8,128)S(1)}, s32[32,32]{1,0:T(8,128)}, u32[]{:S(2)}) copy-start(s32[32,32]{1,0:T(8,128)} %param.22) | copy-start | bytes 12292
  62.6 5.5 %copy-start.6 = (f32[1280]{0:T(1024)S(1)}, f32[1280]{0:T(1024)}, u32[]{:S(2)}) copy-start(f32[1280]{0:T(1024)} %param.19) | copy-start | bytes 15364
  62.6 5.5 %copy-start.3 = (bf16[384,448]{0,1:T(8,128)(2,1)S(1)}, bf16[384,448]{0,1:T(8,128)(2,1)}, u32[]{:S(2)}) copy-start(bf16[384,448]{0,1:T(8,128)(2,1)} %param.21) | copy-start | bytes 1032196
  63.9 38.3 %all-to-all-start.1 = ((bf16[8,64,1280]{2,1,0:T(8,128)(2,1)}), bf16[8,64,1280]{2,1,0:T(8,128)(2,1)S(1)}, u32[]{:S(2)}, u32[]{:S(2)}) async-start(bf16[8,64,1280]{2,1,0:T(8,128)(2,1)} %broadcast_in_dim.103), calls=%async_computation.1 | async-start | bytes 2621440 | tf_op jit(solution)/shard_map/all_to_all | solution.py:25
  117.6 25.0 %all-to-all-start.2 = ((bf16[32,32,448]{2,1,0:T(8,128)(2,1)}), bf16[32,32,448]{2,1,0:T(8,128)(2,1)S(1)}, u32[]{:S(2)}, u32[]{:S(2)}) async-start(bf16[32,32,448]{2,1,0:T(8,128)(2,1)} %select_select_fusion), calls=%async_computation.2 | async-start | bytes 2097152 | tf_op jit(solution)/shard_map/all_to_all | solution.py:133
  125.5 212.9 %reduce-scatter.2.cloned.1.call-start = ((), (), s32[]{:S(2)}) async-start(), calls=%async_computation.5 | async-start | bytes 4128768 | tf_op jit(solution)/shard_map/reduce_scatter | solution.py:155
  144.8 14.4 %collective-permute-start = (bf16[512,448]{1,0:T(8,128)(2,1)S(1)}, bf16[512,448]{1,0:T(8,128)(2,1)S(1)}, u32[]{:S(2)}, u32[]{:S(2)}) collective-permute-start(bf16[512,448]{1,0:T(8,128)(2,1)S(1)} %broadcast_select_fusion), channel_id=1, source_target_pairs={{0,1},{1,2},{2,3},{3,4},{4,5},{5,6},{6,7},{7,0},{8,9},{9,10},{10,1... | collective-permute-start | bytes 1376264 | tf_op jit(solution)/shard_map/ppermute | solution.py:83
  159.2 13.4 %collective-permute-start.1 = (bf16[512,448]{1,0:T(8,128)(2,1)S(1)}, bf16[512,448]{1,0:T(8,128)(2,1)S(1)}, u32[]{:S(2)}, u32[]{:S(2)}) collective-permute-start(bf16[512,448]{1,0:T(8,128)(2,1)S(1)} %collective-permute-done), channel_id=1, source_target_pairs={{0,1},{1,2},{2,3},{3,4},{4,5},{5,6},{6,7},{7,0},{8,9},{9,10},{10,1... | collective-permute-start | bytes 1376264 | tf_op jit(solution)/shard_map/ppermute | solution.py:83
  172.6 12.5 %collective-permute-start.2 = (bf16[512,448]{1,0:T(8,128)(2,1)S(1)}, bf16[512,448]{1,0:T(8,128)(2,1)S(1)}, u32[]{:S(2)}, u32[]{:S(2)}) collective-permute-start(bf16[512,448]{1,0:T(8,128)(2,1)S(1)} %collective-permute-done.1), channel_id=1, source_target_pairs={{0,1},{1,2},{2,3},{3,4},{4,5},{5,6},{6,7},{7,0},{8,9},{9,10},{10,1... | collective-permute-start | bytes 1376264 | tf_op jit(solution)/shard_map/ppermute | solution.py:83
  185.1 11.6 %collective-permute-start.3 = (bf16[512,448]{1,0:T(8,128)(2,1)S(1)}, bf16[512,448]{1,0:T(8,128)(2,1)S(1)}, u32[]{:S(2)}, u32[]{:S(2)}) collective-permute-start(bf16[512,448]{1,0:T(8,128)(2,1)S(1)} %collective-permute-done.2), channel_id=1, source_target_pairs={{0,1},{1,2},{2,3},{3,4},{4,5},{5,6},{6,7},{7,0},{8,9},{9,10},{10,1... | collective-permute-start | bytes 1376264 | tf_op jit(solution)/shard_map/ppermute | solution.py:83
  196.6 10.6 %collective-permute-start.4 = (bf16[512,448]{1,0:T(8,128)(2,1)S(1)}, bf16[512,448]{1,0:T(8,128)(2,1)S(1)}, u32[]{:S(2)}, u32[]{:S(2)}) collective-permute-start(bf16[512,448]{1,0:T(8,128)(2,1)S(1)} %collective-permute-done.3), channel_id=1, source_target_pairs={{0,1},{1,2},{2,3},{3,4},{4,5},{5,6},{6,7},{7,0},{8,9},{9,10},{10,1... | collective-permute-start | bytes 1376264 | tf_op jit(solution)/shard_map/ppermute | solution.py:83
  207.2 10.5 %collective-permute-start.5 = (bf16[512,448]{1,0:T(8,128)(2,1)S(1)}, bf16[512,448]{1,0:T(8,128)(2,1)}, u32[]{:S(2)}, u32[]{:S(2)}) collective-permute-start(bf16[512,448]{1,0:T(8,128)(2,1)S(1)} %collective-permute-done.4), channel_id=1, source_target_pairs={{0,1},{1,2},{2,3},{3,4},{4,5},{5,6},{6,7},{7,0},{8,9},{9,10},{10,1... | collective-permute-start | bytes 1376264 | tf_op jit(solution)/shard_map/ppermute | solution.py:83
  217.7 10.7 %collective-permute-start.6 = (bf16[512,448]{1,0:T(8,128)(2,1)}, bf16[512,448]{1,0:T(8,128)(2,1)}, u32[]{:S(2)}, u32[]{:S(2)}) collective-permute-start(bf16[512,448]{1,0:T(8,128)(2,1)} %collective-permute-done.5), channel_id=1, source_target_pairs={{0,1},{1,2},{2,3},{3,4},{4,5},{5,6},{6,7},{7,0},{8,9},{9,10},{10,1... | collective-permute-start | bytes 1376264 | tf_op jit(solution)/shard_map/ppermute | solution.py:83
  240.0 5.3 %copy-start.7 = (f32[3584]{0:T(1024)S(1)}, f32[3584]{0:T(1024)}, u32[]{:S(2)}) copy-start(f32[3584]{0:T(1024)} %param.24) | copy-start | bytes 43012
  269.7 70.9 %copy-start.1 = (bf16[160,1280]{1,0:T(8,128)(2,1)S(1)}, bf16[160,1280]{1,0:T(8,128)(2,1)}, u32[]{:S(2)}) copy-start(bf16[160,1280]{1,0:T(8,128)(2,1)} %param.18) | copy-start | bytes 1228804
Sparse Core Ops, SparseCore 0:
  9.9 102.6 all-gather.1
  285.7 52.6 reduce-scatter.1
